TPU v7x, 32 devices: a whole 2x2x4 slice. The times are simulated.
32 devices in a mesh: dom: 16 (over z, x, core), col: 2 (over y).
Axes of the slice: x: 2, y: 2, z: 4, core: 2. Of those that a mesh axis runs over, the one named last changes fastest.
Arguments:
- feats: bfloat16 [8192, 256], P('dom', 'col'), may hold values from -6 to 6
- w_first: bfloat16 [256, 256], replicated, may hold values from -0.375 to 0.375
- w_second: bfloat16 [256, 256], replicated, may hold values from -0.375 to 0.375
- block_cols: int32 [64, 32], P('dom'), may hold values from 0 to 63, as said below
- block_count: int32 [64], P('dom'), may hold values from 1 to 32
- block_vals: bfloat16 [64, 32, 128, 128], P('dom', 'col'), may hold values from -0.125 to 0.125
- cotangent: bfloat16 [8192, 256], P('dom', 'col'), may hold values from -6 to 6
Outputs:
- output: float32 [8192, 256], P('dom', 'col')
- grad_first: float32 [256, 256], P(None, 'col')
- grad_second: float32 [256, 256], P(None, 'col')
Inputs may be any that keep to these rules, and one draw needn't show every extreme that they name: Each row of block_cols names 32 different column blocks.
All inputs are finite; a program needn't handle non-finite values.
Results may differ from a plain program's by a relative error of at most 0.019.
Values may be sent and summed in bfloat16 or wider, within the bound.
No kernel may reach another device: no remote copies, remote signals or barrier semaphores. Data moves between devices by JAX's collectives and lax.ppermute only.
A program may use at most 64 MiB of HBM per device.

v0:
```python
import jax
import jax.numpy as jnp
from jax import lax
from jax.sharding import PartitionSpec as P

BLK = 128


def silu_slope(value):
    sig = jax.nn.sigmoid(value)
    return sig + value * sig * (1.0 - sig)


def forward_fold(prod, cols, vals):
    rows, width = prod.shape
    piece = lax.all_gather(prod, "dom", axis=0, tiled=True)
    count_blocks = piece.shape[0] // BLK
    hit = (cols >= 0) & (cols < count_blocks)
    picked = piece.reshape(count_blocks, BLK, width)[jnp.clip(cols, 0, count_blocks - 1)]
    picked = jnp.where(hit[:, :, None, None], picked, jnp.zeros((), picked.dtype))
    contrib = jnp.einsum("rkij,rkjf->rif", vals, picked, preferred_element_type=jnp.float32)
    return contrib.reshape(rows, width)


def backward_scatter(grad, cols, vals):
    rows, width = grad.shape
    nblocks = rows // BLK
    products = jnp.einsum(
        "rkij,rif->rkjf",
        vals,
        grad.reshape(nblocks, BLK, width),
        preferred_element_type=jnp.float32,
    )
    count = rows * lax.axis_size("dom")
    count_blocks = count // BLK
    onehot = (cols[:, :, None] == jnp.arange(count_blocks)[None, None, :]).astype(jnp.float32)
    summed = jnp.einsum("rkp,rkjf->pjf", onehot, products, precision=lax.Precision.HIGHEST)
    return lax.psum_scatter(summed.reshape(count, width), "dom", scatter_dimension=0, tiled=True)


def body(feats, w_first, w_second, block_cols, block_count, block_vals, cotangent):
    col_index = lax.axis_index("col")
    rows, narrow = feats.shape

    def widen(value):
        return lax.all_gather(value, "col", axis=1, tiled=True)

    def weight_grad(full, back):
        return lax.psum(
            jnp.dot(full.T, back, preferred_element_type=jnp.float32).astype(jnp.bfloat16), "dom"
        ).astype(jnp.float32)

    all_vals = lax.all_gather(block_vals, "col", axis=1, tiled=True)
    slot_ids = jnp.arange(all_vals.shape[1])
    usable = slot_ids[None, :] < block_count[:, None]
    vals = jnp.where(usable[:, :, None, None], all_vals, jnp.zeros((), all_vals.dtype))

    def project(full, weight):
        weight_cols = lax.dynamic_slice_in_dim(weight, col_index * narrow, narrow, 1)
        return jnp.dot(full, weight_cols, preferred_element_type=jnp.float32).astype(jnp.bfloat16)

    def aggregate(prod):
        return forward_fold(prod, block_cols, vals)

    def transpose(grad):
        return backward_scatter(grad, block_cols, vals)

    full_input = widen(feats)
    first = aggregate(project(full_input, w_first))
    hidden = (first * jax.nn.sigmoid(first)).astype(jnp.bfloat16)
    full_hidden = widen(hidden)
    output = aggregate(project(full_hidden, w_second))
    back_second = transpose(cotangent).astype(jnp.bfloat16)
    grad_second = weight_grad(full_hidden, back_second)
    second_cols = lax.dynamic_slice_in_dim(w_second, col_index * narrow, narrow, 1)
    partial_hidden = jnp.dot(back_second, second_cols.T, preferred_element_type=jnp.float32)
    hidden_grad = lax.psum_scatter(partial_hidden, "col", scatter_dimension=1, tiled=True)
    act_grad = (hidden_grad * silu_slope(first)).astype(jnp.bfloat16)
    back_first = transpose(act_grad).astype(jnp.bfloat16)
    grad_first = weight_grad(full_input, back_first)
    return (output, grad_first, grad_second)


def solution(mesh):
    in_specs = (
        P("dom", "col"),
        P(),
        P(),
        P("dom", None),
        P("dom"),
        P("dom", "col", None, None),
        P("dom", "col"),
    )
    out_specs = (P("dom", "col"), P(None, "col"), P(None, "col"))
    return jax.shard_map(body, mesh=mesh, in_specs=in_specs, out_specs=out_specs, check_vma=False)
```

profile of v0, /device:TPU:8, one launch (start us, length us, event | category | flops | bytes accessed | tf_op | source)
XLA Modules:
  0.0 452.0 jit_solution(4109258928189561779)
XLA Ops:
  8.7 58.8 %all-gather.4.cloned.1.call-done = bf16[4,32,128,128]{3,2,1,0:T(8,128)(2,1)} async-done(((bf16[4,16,128,128]{3,2,1,0:T(8,128)(2,1)}), bf16[4,32,128,128]{3,2,1,0:T(8,128)(2,1)}) %all-gather.4.cloned.1.call-update) | async-done | bytes 4194320 | tf_op jit(solution)/shard_map/all_gather | solution.py:53
  67.4 4.5 broadcast_select_fusion
  71.9 7.9 %copy.18 = bf16[4,32,128,128]{2,1,0,3:T(8,128)(2,1)} copy(bf16[4,32,128,128]{3,2,1,0:T(8,128)(2,1)} %broadcast_select_fusion) | data formatting | bytes 8388608 | tf_op jit(solution)/shard_map/jit(_where)/select_n | solution.py:56
  79.9 3.4 fusion.31
  83.3 3.9 convolution_bitcast_fusion.1
  87.3 4.4 copy.13
  91.8 0.8 copy-done.2
  92.6 5.8 %all_gather.16 = bf16[512,256]{1,0:T(8,128)(2,1)S(1)} all-gather(bf16[512,128]{1,0:T(8,128)(2,1)S(1)} %copy-done.2), channel_id=1, replica_groups=mesh['dom'=16,'col'=2] {'col'}, dimensions={1}, use_global_device_ids=true | all-gather | bytes 393216 | tf_op jit(solution)/shard_map/all_gather | solution.py:46
  98.4 0.9 fusion.8
  99.3 64.6 %reduce-scatter.4.cloned.1.call-done = f32[512,128]{1,0:T(8,128)} async-done(((f32[8192,128]{1,0:T(8,128)}), f32[512,128]{1,0:T(8,128)}) %reduce-scatter.4.cloned.1.call-update) | async-done | bytes 262160 | tf_op jit(solution)/shard_map/reduce_scatter | solution.py:38
  163.9 2.0 fusion.16
  166.1 40.7 %all-gather.6.cloned.1.call-done = bf16[8192,128]{0,1:T(8,128)(2,1)} async-done(((bf16[512,128]{0,1:T(8,128)(2,1)}), bf16[8192,128]{0,1:T(8,128)(2,1)}) %all-gather.6.cloned.1.call-update) | async-done | bytes 2097168 | tf_op jit(solution)/shard_map/all_gather | solution.py:16
  206.8 3.2 copy.21
  210.0 3.0 gather_fusion
  213.0 5.0 %fusion.2 = f32[4,128,128,1]{2,1,3,0:T(8,128)S(1)} fusion(bf16[4,32,128,128]{3,2,1,0:T(8,128)(2,1)} %broadcast_select_fusion, bf16[4,32,128,128]{3,2,1,0:T(8,128)(2,1)} %bitcast.68, pred[4,32]{1,0:T(4,128)(4,1)S(1)} %compare_and_fusion), kind=kOutput, calls=%fused_computation.4 | convolution fusion | flops 538968064 | bytes 8650880 | tf_op jit(solution)/shard_map/rkij,rkjf->rif/dot_general | solution.py:21
  218.0 5.3 %reduce-scatter.6.cloned.1.call-done = f32[512,128]{1,0:T(8,128)} async-done(((f32[512,256]{1,0:T(8,128)}), f32[512,128]{1,0:T(8,128)}) %reduce-scatter.6.cloned.1.call-update) | async-done | bytes 262160 | tf_op jit(solution)/shard_map/reduce_scatter | solution.py:77
  223.3 1.1 multiply_convert_fusion
  224.4 5.8 %all_gather.18 = bf16[512,256]{1,0:T(8,128)(2,1)S(1)} all-gather(bf16[512,128]{1,0:T(8,128)(2,1)S(1)} %get-tuple-element.12), channel_id=1, replica_groups=mesh['dom'=16,'col'=2] {'col'}, dimensions={1}, use_global_device_ids=true | all-gather | bytes 393216 | tf_op jit(solution)/shard_map/all_gather | solution.py:46
  230.2 0.9 convolution_convert_fusion
  231.3 3.4 fusion.32
  234.8 3.9 convolution_bitcast_fusion
  238.7 4.4 copy.14
  243.2 0.9 copy-done.1
  244.1 0.9 convolution_convert_fusion.2
  245.0 26.6 %all-gather.8.cloned.1.call-done = bf16[8192,128]{1,0:T(8,128)(2,1)} async-done(((bf16[512,128]{1,0:T(8,128)(2,1)}), bf16[8192,128]{1,0:T(8,128)(2,1)}) %all-gather.8.cloned.1.call-update) | async-done | bytes 2097168 | tf_op jit(solution)/shard_map/all_gather | solution.py:16
  271.6 4.7 %gather_fusion.1 = bf16[128,128,128]{2,1,0:T(8,128)(2,1)} fusion(bf16[64,128,128]{2,1,0:T(8,128)(2,1)} %bitcast.66, s32[1024]{0:T(1024)S(1)} %pad_clamp_fusion), kind=kCustom, calls=%fused_computation.1 | custom fusion | bytes 8389120 | tf_op jit(solution)/shard_map/gather | solution.py:19
  276.2 71.0 %reduce-scatter.8.cloned.1.call-done = f32[512,128]{1,0:T(8,128)} async-done(((f32[8192,128]{1,0:T(8,128)}), f32[512,128]{1,0:T(8,128)}) %reduce-scatter.8.cloned.1.call-update) | async-done | bytes 262160 | tf_op jit(solution)/shard_map/reduce_scatter | solution.py:38
  347.3 1.8 fusion.9
  349.1 5.5 %fusion = f32[4,128,128,1]{2,1,3,0:T(8,128)} fusion(bf16[4,32,128,128]{3,2,1,0:T(8,128)(2,1)} %broadcast_select_fusion, bf16[4,32,128,128]{3,2,1,0:T(8,128)(2,1)} %bitcast.67, pred[4,32]{1,0:T(4,128)(4,1)S(1)} %compare_and_fusion), kind=kOutput, calls=%fused_computation.2 | convolution fusion | flops 538968064 | bytes 8650880 | tf_op jit(solution)/shard_map/rkij,rkjf->rif/dot_general | solution.py:21
  354.6 87.5 %all-reduce.3.cloned.1.call-done = (bf16[256,128]{0,1:T(8,128)(2,1)}, bf16[256,128]{1,0:T(8,128)(2,1)}) async-done(((bf16[256,128]{0,1:T(8,128)(2,1)}, bf16[256,128]{1,0:T(8,128)(2,1)}), (bf16[256,128]{0,1:T(8,128)(2,1)}, bf16[256,128]{1,0:T(8,128)(2,1)})) %all-reduce.3.cloned.1.call-update) | async-done | bytes 131088 | tf_op jit(solution)/shard_map/psum | solution.py:49
  442.1 1.6 copy.15
  443.7 1.5 convert_element_type.49
  (29 shorter events, 2.1 us)
Async XLA Ops:
  7.2 72.7 %copy-start = (bf16[512,128]{1,0:T(8,128)(2,1)S(1)}, bf16[512,128]{1,0:T(8,128)(2,1)}, u32[]{:S(2)}) copy-start(bf16[512,128]{1,0:T(8,128)(2,1)} %param.13) | copy-start | bytes 393220
  7.2 60.3 %all-gather.4.cloned.1.call-start = ((), (), s32[]{:S(2)}) async-start(), calls=%async_computation.3 | async-start | bytes 6291456 | tf_op jit(solution)/shard_map/all_gather | solution.py:53
  7.9 156.0 %reduce-scatter.4.cloned.1.call-start = ((), (), s32[]{:S(2)}) async-start(), calls=%async_computation.6 | async-start | bytes 4456448 | tf_op jit(solution)/shard_map/reduce_scatter | solution.py:38
  79.9 3.4 copy-start.5
  91.7 0.9 copy-start.2
  91.7 6.7 %copy-start.4 = (bf16[256,256]{1,0:T(8,128)(2,1)S(1)}, bf16[256,256]{1,0:T(8,128)(2,1)}, u32[]{:S(2)}) copy-start(bf16[256,256]{1,0:T(8,128)(2,1)} %param.8) | copy-start | bytes 393220
  91.7 72.2 %copy-start.3 = (bf16[256,256]{1,0:T(8,128)(2,1)S(1)}, bf16[256,256]{1,0:T(8,128)(2,1)}, u32[]{:S(2)}) copy-start(bf16[256,256]{1,0:T(8,128)(2,1)} %param.9) | copy-start | bytes 393220
  91.7 115.1 %all-gather.6.cloned.1.call-start = ((), (), s32[]{:S(2)}) async-start(), calls=%async_computation.4 | async-start | bytes 2228224 | tf_op jit(solution)/shard_map/all_gather | solution.py:16
  99.3 124.0 %reduce-scatter.6.cloned.1.call-start = ((), (), s32[]{:S(2)}) async-start(), calls=%async_computation.7 | async-start | bytes 786432 | tf_op jit(solution)/shard_map/reduce_scatter | solution.py:77
  165.9 105.6 %all-gather.8.cloned.1.call-start = ((), (), s32[]{:S(2)}) async-start(), calls=%async_computation.5 | async-start | bytes 2228224 | tf_op jit(solution)/shard_map/all_gather | solution.py:16
  231.1 116.2 %reduce-scatter.8.cloned.1.call-start = ((), (), s32[]{:S(2)}) async-start(), calls=%async_computation.8 | async-start | bytes 4456448 | tf_op jit(solution)/shard_map/reduce_scatter | solution.py:38
  243.1 0.9 copy-start.1
  243.1 199.0 %all-reduce.3.cloned.1.call-start = ((), (), s32[]{:S(2)}) async-start(), calls=%async_computation.9 | async-start | bytes 262144 | tf_op jit(solution)/shard_map/psum | solution.py:49
Sparse Core Ops, SparseCore 0:
  9.5 57.8 all-gather.3
  91.8 72.0 reduce-scatter.3
  166.7 40.0 all-gather.5
  208.8 14.4 reduce-scatter.5
  231.2 40.2 all-gather.7
  275.3 71.9 reduce-scatter.7
  351.4 90.6 all-reduce.2
where the time goes:
time: 453 us; the launch traced here: 452 us
  waiting for transfers between devices  355 us (78%)
  matrix products  31.6 us (7%)
  local copies, waits for them, and re-layouts  31 us (7%)
  between operations  14.2 us (3%)
  blocking collectives  11.6 us (3%)
  other arithmetic  7.83 us (2%)
    reduce_scatter x2, waiting for transfers between devices, backward_scatter(): lax.psum_scatter(summed.reshape(count, width), 'dom', scatter_dimension=0...  136 us
    psum x1, waiting for transfers between devices, weight_grad(): lax.psum(jnp.dot(full.T, back, preferred_element_type=jnp.float32).astype...  87.5 us
    all_gather x2, waiting for transfers between devices, forward_fold(): piece = lax.all_gather(prod, 'dom', axis=0, tiled=True)  67.3 us
    all_gather x1, waiting for transfers between devices, body(): all_vals = lax.all_gather(block_vals, 'col', axis=1, tiled=True)  58.8 us
    all_gather x2, blocking collectives, widen(): return lax.all_gather(value, 'col', axis=1, tiled=True)  11.6 us
    dot_general x2, matrix products, forward_fold(): jnp.einsum('rkij,rkjf->rif', vals, picked, preferred_element_type=jnp.flo...  10.4 us
  transfers between devices with their start and end apart: 7, of which 7 were waited for; matrix products, arithmetic and copies ran while one was open for 8% of the time, Pallas kernels for 0%

commit v1 on v0

--- a/solution.py
+++ b/solution.py
@@ -2,6 +2,7 @@
 import jax.numpy as jnp
 from jax import lax
 from jax.sharding import PartitionSpec as P
+from jax.lax import all_gather
 
 BLK = 128
 
@@ -46,8 +47,13 @@
         return lax.all_gather(value, "col", axis=1, tiled=True)
 
     def weight_grad(full, back):
-        return lax.psum(
-            jnp.dot(full.T, back, preferred_element_type=jnp.float32).astype(jnp.bfloat16), "dom"
+
+        def lead_rows(local_block):
+            odd = all_gather(local_block, axis_name="dom")
+            return jnp.sum(odd, axis=0)
+
+        return lead_rows(
+            jnp.dot(full.T, back, preferred_element_type=jnp.float32).astype(jnp.bfloat16)
         ).astype(jnp.float32)
 
     all_vals = lax.all_gather(block_vals, "col", axis=1, tiled=True)

time: 453 us -> 441 us (0.974)
  waiting for transfers between devices: 355 us -> 341 us
    psum x1 -> x0, waiting for transfers between devices: 87.5 us -> none  [weight_grad(): lax.psum(jnp.dot(full.T, back, preferred_element_type=jnp.float32).astype...]
    all_gather x0 -> x2, waiting for transfers between devices: none -> 65.8 us  [lead_rows(): odd = all_gather(local_block, axis_name='dom')]
    all_gather x2, waiting for transfers between devices: 67.3 us -> 81.4 us  [forward_fold(): piece = lax.all_gather(prod, 'dom', axis=0, tiled=True)]
    reduce_scatter x2, waiting for transfers between devices: 136 us -> 129 us  [backward_scatter(): lax.psum_scatter(summed.reshape(count, width), 'dom', scatter_dimension=0...]
  transfers between devices with their start and end apart: 7 -> 8, of which waited for: 7 -> 8; matrix products, arithmetic and copies ran while one was open for 8% -> 7% of each run, Pallas kernels for 0% -> 0%
where the time goes in v1:
time: 441 us; the launch traced here: 439 us
  waiting for transfers between devices  341 us (77%)
  matrix products  31.7 us (7%)
  local copies, waits for them, and re-layouts  30.8 us (7%)
  between operations  14.2 us (3%)
  blocking collectives  11.6 us (3%)
  other arithmetic  8.89 us (2%)
    reduce_scatter x2, waiting for transfers between devices, backward_scatter(): lax.psum_scatter(summed.reshape(count, width), 'dom', scatter_dimension=0...  129 us
    all_gather x2, waiting for transfers between devices, forward_fold(): piece = lax.all_gather(prod, 'dom', axis=0, tiled=True)  81.4 us
    all_gather x2, waiting for transfers between devices, lead_rows(): odd = all_gather(local_block, axis_name='dom')  65.8 us
    all_gather x1, waiting for transfers between devices, body(): all_vals = lax.all_gather(block_vals, 'col', axis=1, tiled=True)  58.8 us
    all_gather x2, blocking collectives, widen(): return lax.all_gather(value, 'col', axis=1, tiled=True)  11.6 us
    dot_general x2, matrix products, forward_fold(): jnp.einsum('rkij,rkjf->rif', vals, picked, preferred_element_type=jnp.flo...  10.5 us
  transfers between devices with their start and end apart: 8, of which 8 were waited for; matrix products, arithmetic and copies ran while one was open for 7% of the time, Pallas kernels for 0%

profile of v1, /device:TPU:8, one launch (start us, length us, event | category | flops | bytes accessed | tf_op | source)
XLA Modules:
  0.0 439.0 jit_solution(6425169477652479655)
XLA Ops:
  8.7 58.8 %all-gather.8.cloned.1.call-done = bf16[4,32,128,128]{3,2,1,0:T(8,128)(2,1)} async-done(((bf16[4,16,128,128]{3,2,1,0:T(8,128)(2,1)}), bf16[4,32,128,128]{3,2,1,0:T(8,128)(2,1)}) %all-gather.8.cloned.1.call-update) | async-done | bytes 4194320 | tf_op jit(solution)/shard_map/all_gather | solution.py:59
  67.4 4.5 %broadcast_select_fusion = bf16[4,32,128,128]{3,2,1,0:T(8,128)(2,1)} fusion(bf16[4,32,128,128]{3,2,1,0:T(8,128)(2,1)} %all-gather.8.cloned.1.call-done, pred[4,32]{1,0:T(4,128)(4,1)S(1)} %iota_compare_fusion.1), kind=kLoop, calls=%fused_computation.8 | loop fusion | flops 2097152 | bytes 8388736 | tf_op jit(solution)/shard_map/jit(_where)/select_n | solution.py:62
  72.0 7.9 %copy.17 = bf16[4,32,128,128]{2,1,0,3:T(8,128)(2,1)} copy(bf16[4,32,128,128]{3,2,1,0:T(8,128)(2,1)} %broadcast_select_fusion) | data formatting | bytes 8388608 | tf_op jit(solution)/shard_map/jit(_where)/select_n | solution.py:62
  79.9 3.4 fusion.31
  83.4 3.9 convolution_bitcast_fusion.1
  87.3 4.4 %copy.16 = f32[64,128,128]{2,1,0:T(8,128)} copy(f32[64,128,128]{2,0,1:T(8,128)S(1)} %convolution_bitcast_fusion.1) | data formatting | bytes 8388608 | tf_op jit(solution)/shard_map/rkp,rkjf->pjf/dot_general | solution.py:38
  91.8 0.8 copy-done.3
  92.6 5.8 %all_gather.28 = bf16[512,256]{1,0:T(8,128)(2,1)S(1)} all-gather(bf16[512,128]{1,0:T(8,128)(2,1)S(1)} %copy-done.3), channel_id=1, replica_groups=mesh['dom'=16,'col'=2] {'col'}, dimensions={1}, use_global_device_ids=true | all-gather | bytes 393216 | tf_op jit(solution)/shard_map/all_gather | solution.py:47
  98.4 0.9 fusion.8
  99.3 64.7 %reduce-scatter.4.cloned.1.call-done = f32[512,128]{1,0:T(8,128)} async-done(((f32[8192,128]{1,0:T(8,128)}), f32[512,128]{1,0:T(8,128)}) %reduce-scatter.4.cloned.1.call-update) | async-done | bytes 262160 | tf_op jit(solution)/shard_map/reduce_scatter | solution.py:39
  164.1 2.0 fusion.16
  166.4 40.4 %all-gather.10.cloned.1.call-done = bf16[8192,128]{0,1:T(8,128)(2,1)} async-done(((bf16[512,128]{0,1:T(8,128)(2,1)}), bf16[8192,128]{0,1:T(8,128)(2,1)}) %all-gather.10.cloned.1.call-update) | async-done | bytes 2097168 | tf_op jit(solution)/shard_map/all_gather | solution.py:17
  206.8 3.2 copy.24
  210.0 3.1 gather_fusion
  213.1 5.0 %fusion.2 = f32[4,128,128,1]{2,1,3,0:T(8,128)S(1)} fusion(bf16[4,32,128,128]{3,2,1,0:T(8,128)(2,1)} %broadcast_select_fusion, bf16[4,32,128,128]{3,2,1,0:T(8,128)(2,1)} %bitcast.74, pred[4,32]{1,0:T(4,128)(4,1)S(1)} %compare_and_fusion), kind=kOutput, calls=%fused_computation.4 | convolution fusion | flops 538968064 | bytes 8650880 | tf_op jit(solution)/shard_map/rkij,rkjf->rif/dot_general | solution.py:22
  218.1 5.3 %reduce-scatter.6.cloned.1.call-done = f32[512,128]{1,0:T(8,128)} async-done(((f32[512,256]{1,0:T(8,128)}), f32[512,128]{1,0:T(8,128)}) %reduce-scatter.6.cloned.1.call-update) | async-done | bytes 262160 | tf_op jit(solution)/shard_map/reduce_scatter | solution.py:83
  223.4 1.1 multiply_convert_fusion
  224.4 3.4 fusion.32
  227.9 3.9 convolution_bitcast_fusion
  231.8 4.4 %copy.18 = f32[64,128,128]{2,1,0:T(8,128)} copy(f32[64,128,128]{2,0,1:T(8,128)S(1)} %convolution_bitcast_fusion) | data formatting | bytes 8388608 | tf_op jit(solution)/shard_map/rkp,rkjf->pjf/dot_general | solution.py:38
  236.3 5.8 %all_gather.30 = bf16[512,256]{1,0:T(8,128)(2,1)S(1)} all-gather(bf16[512,128]{1,0:T(8,128)(2,1)S(1)} %get-tuple-element.7), channel_id=1, replica_groups=mesh['dom'=16,'col'=2] {'col'}, dimensions={1}, use_global_device_ids=true | all-gather | bytes 393216 | tf_op jit(solution)/shard_map/all_gather | solution.py:47
  242.1 0.9 convolution_convert_fusion.2
  243.1 0.9 convolution_convert_fusion
  244.3 64.3 %reduce-scatter.8.cloned.1.call-done = f32[512,128]{1,0:T(8,128)} async-done(((f32[8192,128]{1,0:T(8,128)}), f32[512,128]{1,0:T(8,128)}) %reduce-scatter.8.cloned.1.call-update) | async-done | bytes 262160 | tf_op jit(solution)/shard_map/reduce_scatter | solution.py:39
  308.6 1.8 fusion.9
  310.4 37.3 %all-gather.16.cloned.1.call-done = bf16[4096,128]{1,0:T(8,128)(2,1)} async-done(((bf16[256,128]{1,0:T(8,128)(2,1)}), bf16[4096,128]{1,0:T(8,128)(2,1)}) %all-gather.16.cloned.1.call-update) | async-done | bytes 1048592 | tf_op jit(solution)/shard_map/all_gather | solution.py:52
  347.7 1.4 reduce_sum.25
  349.7 41.0 %all-gather.12.cloned.1.call-done = bf16[8192,128]{1,0:T(8,128)(2,1)} async-done(((bf16[512,128]{1,0:T(8,128)(2,1)}), bf16[8192,128]{1,0:T(8,128)(2,1)}) %all-gather.12.cloned.1.call-update) | async-done | bytes 2097168 | tf_op jit(solution)/shard_map/all_gather | solution.py:17
  390.8 4.6 %gather_fusion.1 = bf16[128,128,128]{2,1,0:T(8,128)(2,1)} fusion(bf16[64,128,128]{2,1,0:T(8,128)(2,1)} %bitcast.72, s32[1024]{0:T(1024)S(1)} %pad_clamp_fusion), kind=kCustom, calls=%fused_computation.1 | custom fusion | bytes 8389120 | tf_op jit(solution)/shard_map/gather | solution.py:20
  395.4 5.5 %fusion = f32[4,128,128,1]{2,1,3,0:T(8,128)} fusion(bf16[4,32,128,128]{3,2,1,0:T(8,128)(2,1)} %broadcast_select_fusion, bf16[4,32,128,128]{3,2,1,0:T(8,128)(2,1)} %bitcast.73, pred[4,32]{1,0:T(4,128)(4,1)S(1)} %compare_and_fusion), kind=kOutput, calls=%fused_computation.2 | convolution fusion | flops 538968064 | bytes 8650880 | tf_op jit(solution)/shard_map/rkij,rkjf->rif/dot_general | solution.py:22
  400.9 28.5 %all-gather.14.cloned.1.call-done = bf16[4096,128]{0,1:T(8,128)(2,1)} async-done(((bf16[256,128]{0,1:T(8,128)(2,1)}), bf16[4096,128]{0,1:T(8,128)(2,1)}) %all-gather.14.cloned.1.call-update) | async-done | bytes 1048592 | tf_op jit(solution)/shard_map/all_gather | solution.py:52
  429.4 1.5 copy.25
  (37 shorter events, 4.3 us)
Async XLA Ops:
  7.2 72.7 %copy-start = (bf16[512,128]{1,0:T(8,128)(2,1)S(1)}, bf16[512,128]{1,0:T(8,128)(2,1)}, u32[]{:S(2)}) copy-start(bf16[512,128]{1,0:T(8,128)(2,1)} %param.13) | copy-start | bytes 393220
  7.2 60.3 %all-gather.8.cloned.1.call-start = ((), (), s32[]{:S(2)}) async-start(), calls=%async_computation.3 | async-start | bytes 6291456 | tf_op jit(solution)/shard_map/all_gather | solution.py:59
  7.9 156.2 %reduce-scatter.4.cloned.1.call-start = ((), (), s32[]{:S(2)}) async-start(), calls=%async_computation.6 | async-start | bytes 4456448 | tf_op jit(solution)/shard_map/reduce_scatter | solution.py:39
  79.9 3.4 copy-start.6
  91.7 0.9 copy-start.3
  91.7 6.7 %copy-start.5 = (bf16[256,256]{1,0:T(8,128)(2,1)S(1)}, bf16[256,256]{1,0:T(8,128)(2,1)}, u32[]{:S(2)}) copy-start(bf16[256,256]{1,0:T(8,128)(2,1)} %param.8) | copy-start | bytes 393220
  91.7 72.4 %copy-start.4 = (bf16[256,256]{1,0:T(8,128)(2,1)S(1)}, bf16[256,256]{1,0:T(8,128)(2,1)}, u32[]{:S(2)}) copy-start(bf16[256,256]{1,0:T(8,128)(2,1)} %param.9) | copy-start | bytes 393220
  91.7 115.1 %all-gather.10.cloned.1.call-start = ((), (), s32[]{:S(2)}) async-start(), calls=%async_computation.4 | async-start | bytes 2228224 | tf_op jit(solution)/shard_map/all_gather | solution.py:17
  99.3 124.1 %reduce-scatter.6.cloned.1.call-start = ((), (), s32[]{:S(2)}) async-start(), calls=%async_computation.7 | async-start | bytes 786432 | tf_op jit(solution)/shard_map/reduce_scatter | solution.py:83
  166.1 142.5 %reduce-scatter.8.cloned.1.call-start = ((), (), s32[]{:S(2)}) async-start(), calls=%async_computation.8 | async-start | bytes 4456448 | tf_op jit(solution)/shard_map/reduce_scatter | solution.py:39
  236.2 5.9 %copy-start.2 = (f32[512,128]{1,0:T(8,128)S(1)}, f32[512,128]{1,0:T(8,128)}, u32[]{:S(2)}) copy-start(f32[512,128]{1,0:T(8,128)} %reduce-scatter.4.cloned.1.call-done) | copy-start | bytes 786436
  236.2 111.5 %all-gather.16.cloned.1.call-start = ((), (), s32[]{:S(2)}) async-start(), calls=%async_computation.10 | async-start | bytes 1114112 | tf_op jit(solution)/shard_map/all_gather | solution.py:52
  243.0 147.7 %all-gather.12.cloned.1.call-start = ((), (), s32[]{:S(2)}) async-start(), calls=%async_computation.5 | async-start | bytes 2228224 | tf_op jit(solution)/shard_map/all_gather | solution.py:17
  244.0 185.4 %all-gather.14.cloned.1.call-start = ((), (), s32[]{:S(2)}) async-start(), calls=%async_computation.9 | async-start | bytes 1114112 | tf_op jit(solution)/shard_map/all_gather | solution.py:52
  395.4 36.8 %copy-start.1 = (bf16[512,128]{1,0:T(8,128)(2,1)S(1)}, bf16[512,128]{1,0:T(8,128)(2,1)}, u32[]{:S(2)}) copy-start(bf16[512,128]{1,0:T(8,128)(2,1)} %param.13) | copy-start | bytes 393220
Sparse Core Ops, SparseCore 0:
  9.5 57.8 all-gather.7
  91.9 72.1 reduce-scatter.3
  166.8 39.9 all-gather.9
  208.9 14.4 reduce-scatter.5
  236.4 72.1 reduce-scatter.7
  311.2 36.4 all-gather.15
  350.4 40.2 all-gather.11
  392.9 36.4 all-gather.13
